TPU v7x, 32 devices: a whole 2x2x4 slice. The times are simulated.
32 devices in a mesh: parts: 2 (over y), wide: 4 (over z), mp: 4 (over x, core).
Axes of the slice: x: 2, y: 2, z: 4, core: 2. Of those that a mesh axis runs over, the one named last changes fastest.
Arguments:
- prompt_states: bfloat16 [4096, 8192], P(('parts', 'wide'), 'mp'), parts along dimension 0, may hold values from -6 to 6
- norm_gain: float32 [8192], P('mp'), may hold values from 0.1 to 1.9
- kv_weight: bfloat16 [8192, 2048], P('mp', 'wide'), may hold values from -0.0625 to 0.0625
- block_owner: int32 [256, 1], P(('parts', 'wide')), parts along dimension 0, may hold values from 0 to 3; in each aligned block of 32 rows (0 to 31, 32 to 63, ...) at most 16 rows name the same one
- block_request: int32 [256], P(('parts', 'wide')), parts along dimension 0, may hold values from 0 to 1
- block_admit: int32 [256], P(('parts', 'wide')), parts along dimension 0, may hold values 0 or 1
- cache_kv: bfloat16 [16, 2048, 2048], P(('parts', 'wide'), None, 'mp'), parts along dimension 0, may hold values from -6 to 6
- cache_len: int32 [16], P(('parts', 'wide')), parts along dimension 0, may hold values from 1 to 2048
- queries: bfloat16 [16, 4, 8192], P(('parts', 'wide'), None, 'mp'), parts along dimension 0, may hold values from -128 to 128
- draft_kv: bfloat16 [16, 4, 2048], P(('parts', 'wide'), None, 'mp'), parts along dimension 0, may hold values from -8 to 8
Outputs:
- attended: bfloat16 [16, 4, 8192], P(('parts', 'wide'), None, 'mp'), parts along dimension 0
There are 2 independent parts, one for each index of `parts`. A program takes and returns all parts, laid end to end along the dimension named above; an argument that names none is the same for every part. Nothing has to cross between parts.
Inputs may be any that keep to these rules, and one draw needn't show every extreme that they name: `block_owner`: in each prefill group's 32 blocks no owner is named more than 16 times, a bound that some block reaches.
All inputs are finite; a program needn't handle non-finite values. No bound on the sum of `block_admit` on one device may be relied on, other than what follows from the above.
Results may differ from a plain program's by a relative error of at most 0.019.
Values may be sent and summed in bfloat16 or wider, within the bound.
A program may use at most 64 MiB of HBM per device.

v0:
```python
import math

import jax
import jax.numpy as jnp
from jax import lax
from jax.sharding import PartitionSpec as P

D = 8192
KVH = 8
HD = 128
QH = 64
BLK = 16
CACHE = 2048
STEPS = 4


def absorb(state, scores, allowed, values, form):
    highest, total, summed = state
    masked = jnp.where(allowed, scores, -1e30)
    new_top = jnp.maximum(highest, jnp.max(masked, axis=-1))
    weights = jnp.where(allowed, jnp.exp(masked - new_top[..., None]), 0.0)
    shrink = jnp.exp(highest - new_top)
    total = total * shrink + jnp.sum(weights, axis=-1)
    summed = summed * shrink[..., None] + jnp.einsum(
        form, weights, values.astype(jnp.float32), precision=lax.Precision.HIGHEST
    )
    return (new_top, total, summed)


def shared_keys(state, qvec, keys, values, allowed):
    scores = jnp.einsum("rskgd,nkd->rskgn", qvec, keys, preferred_element_type=jnp.float32) * (
        1.0 / math.sqrt(HD)
    )
    return absorb(state, scores, allowed[:, None, None, None, :], values, "rskgn,nkd->rskgd")


def own_keys(state, qvec, keys, values, allowed):
    scores = jnp.einsum("rskgd,rnkd->rskgn", qvec, keys, preferred_element_type=jnp.float32) * (
        1.0 / math.sqrt(HD)
    )
    return absorb(state, scores, allowed, values, "rskgn,rnkd->rskgd")


def on_device(
    prompt_states,
    norm_gain,
    kv_weight,
    block_owner,
    block_request,
    block_admit,
    cache_kv,
    cache_len,
    queries,
    draft_kv,
):
    wide = lax.axis_size("wide")
    states = prompt_states.astype(jnp.float32)
    squares = lax.psum(jnp.sum(states * states, axis=1), "mp")
    inverse = lax.rsqrt(squares / D + 1e-05)
    scaled = (states * norm_gain).astype(jnp.bfloat16)
    partial_kv = jnp.dot(
        scaled,
        lax.all_gather(kv_weight, "wide", axis=1, tiled=True),
        preferred_element_type=jnp.float32,
    )
    rounded_kv = partial_kv.astype(jnp.bfloat16).astype(jnp.float32)
    summed_kv = lax.psum_scatter(
        rounded_kv.astype(jnp.bfloat16), "mp", scatter_dimension=1, tiled=True
    ).astype(jnp.float32)
    prompt_kv = (summed_kv * inverse[:, None]).astype(jnp.bfloat16)
    width = cache_kv.shape[2]
    heads_here = width // (2 * HD)
    groups = QH // KVH
    req_dev = queries.shape[0]
    pblk = block_request.shape[0]
    blocks = prompt_kv.reshape(pblk, BLK, width)
    local_ids = jnp.arange(req_dev, dtype=jnp.int32)
    qvec = queries.reshape(req_dev, STEPS, heads_here, groups, HD)
    state = (
        jnp.full((req_dev, STEPS, heads_here, groups), -1e30, jnp.float32),
        jnp.zeros((req_dev, STEPS, heads_here, groups), jnp.float32),
        jnp.zeros((req_dev, STEPS, heads_here, groups, HD), jnp.float32),
    )
    cached = cache_kv.reshape(req_dev, CACHE, heads_here, 2, HD)
    cache_ok = (jnp.arange(CACHE, dtype=jnp.int32)[None, :] < cache_len[:, None])[
        :, None, None, None, :
    ]
    state = own_keys(state, qvec, cached[:, :, :, 0], cached[:, :, :, 1], cache_ok)
    drafted = draft_kv.reshape(req_dev, STEPS, heads_here, 2, HD)
    step_index = jnp.arange(STEPS, dtype=jnp.int32)
    causal = (step_index[None, :] <= step_index[:, None])[None, :, None, None, :]
    state = own_keys(state, qvec, drafted[:, :, :, 0], drafted[:, :, :, 1], causal)
    owner = block_owner[:, 0]
    capacity = max(2, (2 * pblk + wide - 1) // wide)
    hits = (owner[:, None] == jnp.arange(wide, dtype=jnp.int32)[None, :]).astype(jnp.int32)
    slot = jnp.sum((jnp.cumsum(hits, axis=0) - hits) * hits, axis=1)
    outgoing = jnp.zeros((wide, capacity, BLK, width), jnp.bfloat16).at[owner, slot].set(blocks)
    tagged = jnp.where(block_admit == 1, block_request, -1)
    outgoing_labels = jnp.full((wide, capacity), -1, jnp.int32).at[owner, slot].set(tagged)
    incoming, arrived = (
        lax.all_to_all(outgoing, "wide", split_axis=0, concat_axis=0, tiled=True),
        lax.all_to_all(outgoing_labels, "wide", split_axis=0, concat_axis=0, tiled=True),
    )
    rows = incoming.reshape(-1, heads_here, 2, HD)
    token_labels = jnp.repeat(arrived.reshape(-1), BLK)
    allowed = token_labels[None, :] == local_ids[:, None]
    state = shared_keys(state, qvec, rows[:, :, 0], rows[:, :, 1], allowed)
    highest, total, summed = state
    result = summed / total[..., None]
    return result.reshape(req_dev, STEPS, heads_here * groups * HD).astype(jnp.bfloat16)


def solution(mesh):
    placed = (
        P(("parts", "wide"), "mp"),
        P("mp"),
        P("mp", "wide"),
        P(("parts", "wide"), None),
        P(("parts", "wide")),
        P(("parts", "wide")),
        P(("parts", "wide"), None, "mp"),
        P(("parts", "wide")),
        P(("parts", "wide"), None, "mp"),
        P(("parts", "wide"), None, "mp"),
    )
    return jax.shard_map(
        on_device,
        mesh=mesh,
        in_specs=placed,
        out_specs=P(("parts", "wide"), None, "mp"),
        check_vma=False,
    )
```

profile of v0, /device:TPU:0, one launch (start us, length us, event | category | flops | bytes accessed | tf_op | source)
XLA Modules:
  0.0 251.3 jit_solution(4306500067962030970)
XLA Ops:
  6.5 0.7 all-gather.2.cloned.1.call-update
  7.3 153.9 %all-gather.2.cloned.1.call-done = bf16[2048,2048]{1,0:T(8,128)(2,1)} async-done(((bf16[2048,512]{1,0:T(8,128)(2,1)}), bf16[2048,2048]{1,0:T(8,128)(2,1)}) %all-gather.2.cloned.1.call-update) | async-done | bytes 8388624 | tf_op jit(solution)/shard_map/all_gather | solution.py:63
  161.3 9.9 %convolution_convert_fusion = bf16[512,2048]{1,0:T(8,128)(2,1)} fusion(bf16[2048,2048]{1,0:T(8,128)(2,1)} %all-gather.2.cloned.1.call-done, bf16[512,2048]{1,0:T(8,128)(2,1)} %param.10, f32[2048]{0:T(1024)} %param.11), kind=kOutput, calls=%fused_computation.6 | convolution fusion | flops 4299161600 | bytes 12591104 | tf_op jit(solution)/shard_map/dot_general | solution.py:61
  171.4 0.2 select_reduce_fusion
  171.6 0.6 broadcast_in_dim.109
  172.2 5.3 %scatter_fusion = s32[4,16]{1,0:T(4,128)} fusion(s32[4,16]{1,0:T(4,128)} %broadcast_in_dim.109, s32[32]{0:T(128)S(1)} %fusion.33, s32[32]{0:T(128)S(1)} %compare_select_fusion.2), kind=kCustom, calls=%fused_computation | custom fusion | bytes 640 | tf_op jit(solution)/shard_map/scatter | solution.py:99
  177.5 3.4 %all-to-all-start = ((s32[4,1,16]{2,1,0:T(1,128)}), s32[4,1,16]{2,1,0:T(1,128)S(1)}, u32[]{:S(2)}, u32[]{:S(2)}) async-start(s32[4,1,16]{2,1,0:T(1,128)} %bitcast.22), calls=%async_computation | async-start | bytes 4096 | tf_op jit(solution)/shard_map/all_to_all | solution.py:102
  180.9 0.5 fusion.1
  181.4 7.0 %psum.7 = f32[512]{0:T(512)S(1)} all-reduce(f32[512]{0:T(512)S(1)} %fusion.1), channel_id=1, replica_groups=mesh['parts'=2,'wide'=4,'mp'=4] {'mp'}, use_global_device_ids=true, to_apply=%region_7.8 | all-reduce | flops 512 | bytes 4096 | tf_op jit(solution)/shard_map/psum | solution.py:58
  188.4 12.4 %reduce-scatter.2.cloned.1.call-done = bf16[512,512]{1,0:T(8,128)(2,1)} async-done(((bf16[512,2048]{1,0:T(8,128)(2,1)}), bf16[512,512]{1,0:T(8,128)(2,1)}) %reduce-scatter.2.cloned.1.call-update) | async-done | bytes 524304 | tf_op jit(solution)/shard_map/reduce_scatter | solution.py:67
  200.8 1.2 multiply_convert_fusion
  202.0 1.1 broadcast_in_dim.113
  203.1 4.7 %scatter_fusion.1 = bf16[4,16,16,512]{3,2,1,0:T(8,128)(2,1)} fusion(bf16[4,16,16,512]{3,2,1,0:T(8,128)(2,1)} %broadcast_in_dim.113, s32[32]{0:T(128)S(1)} %fusion.33, bf16[32,16,512]{2,1,0:T(8,128)(2,1)S(1)} %bitcast.108), kind=kCustom, calls=%fused_computation.1 | custom fusion | bytes 1573120 | tf_op jit(solution)/shard_map/scatter | solution.py:97
  207.8 4.5 %all-to-all-start.1 = ((bf16[4,16,16,512]{3,2,1,0:T(8,128)(2,1)}), bf16[4,16,16,512]{3,2,1,0:T(8,128)(2,1)S(1)}, u32[]{:S(2)}, u32[]{:S(2)}) async-start(bf16[4,16,16,512]{3,2,1,0:T(8,128)(2,1)} %scatter_fusion.1), calls=%async_computation.2 | async-start | bytes 2097152 | tf_op jit(solution)/shard_map/all_to_all | solution.py:101
  212.4 6.3 %copy.48 = bf16[2,2048,512]{1,2,0:T(8,128)(2,1)} copy(bf16[2,2048,512]{2,1,0:T(8,128)(2,1)} %param.16) | data formatting | bytes 8388608 | tf_op args[6]
  218.7 0.3 fusion.41
  219.0 0.1 iota_compare_fusion.1
  219.1 2.1 fusion.42
  221.2 0.5 broadcast.144
  221.7 0.7 reduce.3
  222.4 0.1 reshape.141
  222.6 15.3 %all-to-all-done.1 = bf16[4,16,16,512]{3,2,1,0:T(8,128)(2,1)S(1)} async-done(((bf16[4,16,16,512]{3,2,1,0:T(8,128)(2,1)}), bf16[4,16,16,512]{3,2,1,0:T(8,128)(2,1)S(1)}, u32[]{:S(2)}, u32[]{:S(2)}) %all-to-all-start.1) | async-done | bytes 1048608 | tf_op jit(solution)/shard_map/all_to_all | solution.py:101
  237.9 0.3 reshape.143
  238.2 1.5 fusion.39
  239.7 0.4 fusion.40
  240.1 0.2 fusion.37
  240.4 0.3 fusion.19
  240.7 0.1 fusion.27
  240.9 2.1 fusion.15
  243.0 0.3 fusion.13
  243.4 0.4 fusion.16
  243.8 0.6 convert_element_type.36
  (33 shorter events, 0.5 us)
Async XLA Ops:
  6.5 154.7 %all-gather.2.cloned.1.call-start = ((), (), s32[]{:S(2)}) async-start(), calls=%async_computation.3 | async-start | bytes 10485760 | tf_op jit(solution)/shard_map/all_gather | solution.py:63
  7.3 164.0 %copy-start.3 = (s32[32,1]{0,1:T(1,128)S(1)}, s32[32,1]{0,1:T(1,128)}, u32[]{:S(2)}) copy-start(s32[32,1]{0,1:T(1,128)} %param.13) | copy-start | bytes 388
  7.3 164.3 %copy-start.6 = (s32[32]{0:T(128)S(1)}, s32[32]{0:T(128)}, u32[]{:S(2)}) copy-start(s32[32]{0:T(128)} %param.14) | copy-start | bytes 388
  7.3 164.3 %copy-start.7 = (s32[32]{0:T(128)S(1)}, s32[32]{0:T(128)}, u32[]{:S(2)}) copy-start(s32[32]{0:T(128)} %param.15) | copy-start | bytes 388
  7.3 193.5 %reduce-scatter.2.cloned.1.call-start = ((), (), s32[]{:S(2)}) async-start(), calls=%async_computation.4 | async-start | bytes 2621440 | tf_op jit(solution)/shard_map/reduce_scatter | solution.py:67
  171.2 9.7 %copy-start.1 = (bf16[512,2048]{1,0:T(8,128)(2,1)S(1)}, bf16[512,2048]{1,0:T(8,128)(2,1)}, u32[]{:S(2)}) copy-start(bf16[512,2048]{1,0:T(8,128)(2,1)} %param.10) | copy-start | bytes 6291460
  177.5 34.9 %copy-start.2 = (bf16[2,4,2048]{2,1,0:T(4,128)(2,1)S(1)}, bf16[2,4,2048]{2,1,0:T(4,128)(2,1)}, u32[]{:S(2)}) copy-start(bf16[2,4,2048]{2,1,0:T(4,128)(2,1)} %param.18) | copy-start | bytes 98308
  177.5 30.3 %all-to-all-start = ((s32[4,1,16]{2,1,0:T(1,128)}), s32[4,1,16]{2,1,0:T(1,128)S(1)}, u32[]{:S(2)}, u32[]{:S(2)}) async-start(s32[4,1,16]{2,1,0:T(1,128)} %bitcast.22), calls=%async_computation | async-start | bytes 4096 | tf_op jit(solution)/shard_map/all_to_all | solution.py:102
  207.8 30.1 %all-to-all-start.1 = ((bf16[4,16,16,512]{3,2,1,0:T(8,128)(2,1)}), bf16[4,16,16,512]{3,2,1,0:T(8,128)(2,1)S(1)}, u32[]{:S(2)}, u32[]{:S(2)}) async-start(bf16[4,16,16,512]{3,2,1,0:T(8,128)(2,1)} %scatter_fusion.1), calls=%async_computation.2 | async-start | bytes 2097152 | tf_op jit(solution)/shard_map/all_to_all | solution.py:101
  212.4 6.3 %copy-start.5 = (bf16[2,4,512]{2,1,0:T(4,128)(2,1)S(1)}, bf16[2,4,512]{2,1,0:T(4,128)(2,1)}, u32[]{:S(2)}) copy-start(bf16[2,4,512]{2,1,0:T(4,128)(2,1)} %param.19) | copy-start | bytes 24580
  212.4 6.6 %copy-start.4 = (s32[2]{0:T(128)S(1)}, s32[2]{0:T(128)}, u32[]{:S(2)}) copy-start(s32[2]{0:T(128)} %param.17) | copy-start | bytes 28
  238.2 2.7 %copy-start = (bf16[2,2048,512]{1,2,0:T(8,128)(2,1)S(1)}, bf16[2,2048,512]{1,2,0:T(8,128)(2,1)}, u32[]{:S(2)}) copy-start(bf16[2,2048,512]{1,2,0:T(8,128)(2,1)} %copy.48) | copy-start | bytes 12582916
Sparse Core Ops, SparseCore 0:
  8.9 152.3 all-gather.1
  171.3 29.4 reduce-scatter.1
where the time goes:
time: 252 us; the launch traced here: 251 us
  waiting for transfers between devices  182 us (72%)
  local copies, waits for them, and re-layouts  21.3 us (8%)
  matrix products  15.6 us (6%)
  between operations  13.6 us (5%)
  starting transfers between devices  7.94 us (3%)
  blocking collectives  7.02 us (3%)
  other arithmetic  3.51 us (1%)
    all_gather x1, waiting for transfers between devices, on_device(): lax.all_gather(kv_weight, 'wide', axis=1, tiled=True)  154 us
    all_to_all x1, waiting for transfers between devices, on_device(): lax.all_to_all(outgoing, 'wide', split_axis=0, concat_axis=0, tiled=True)  15.3 us
    reduce_scatter x1, waiting for transfers between devices, on_device(): lax.psum_scatter(rounded_kv.astype(jnp.bfloat16), 'mp', scatter_dimension...  12.4 us
    dot_general x1, matrix products, on_device(): jnp.dot(scaled, lax.all_gather(kv_weight, 'wide', axis=1, tiled=True), pr...  9.92 us
    psum x1, blocking collectives, on_device(): squares = lax.psum(jnp.sum(states * states, axis=1), 'mp')  7.02 us
    unnamed x17, local copies, waits for them, and re-layouts  6.33 us
    scatter x1, local copies, waits for them, and re-layouts, on_device(): jnp.full((wide, capacity), -1, jnp.int32).at[owner, slot].set(tagged)  5.34 us
  transfers between devices with their start and end apart: 4, of which 3 were waited for; matrix products, arithmetic and copies ran while one was open for 10% of the time, Pallas kernels for 0%

commit v1 on v0

--- a/solution.py
+++ b/solution.py
@@ -1,8 +1,11 @@
+import functools
 import math
 
 import jax
 import jax.numpy as jnp
 from jax import lax
+from jax.experimental import pallas as pl
+from jax.experimental.pallas import tpu as pltpu
 from jax.sharding import PartitionSpec as P
 
 D = 8192
@@ -110,6 +113,469 @@
     return result.reshape(req_dev, STEPS, heads_here * groups * HD).astype(jnp.bfloat16)
 
 
+LANES = 128
+
+
+def fused_kernel(
+    sizes,
+    x_any,
+    gain_ref,
+    w_any,
+    label_ref,
+    cache_any,
+    len_ref,
+    q_ref,
+    draft_ref,
+    out_ref,
+    xbuf,
+    wbuf,
+    part,
+    gathered,
+    squares_here,
+    squares,
+    inverse,
+    kvbuf,
+    cache_buf,
+    q_all,
+    state_cache,
+    state_out,
+    state_in,
+    local_sem,
+    own_sem,
+    right_send,
+    left_send,
+    z_recv,
+    y_send,
+    y_recv,
+    q_send,
+    q_recv,
+    sq_send,
+    sq_recv,
+    rs_send,
+    rs_recv,
+    st_send,
+    st_recv,
+):
+    n, m_count, rounds, heads, req_dev = sizes
+    w = lax.axis_index("wide")
+    me = lax.axis_index("mp")
+    side = lax.axis_index("parts")
+    tokens, depth = xbuf.shape
+    half = depth // 2
+    rows = q_ref.shape[1]
+    per_req = rows // req_dev
+    scale = 1.0 / math.sqrt(HD)
+
+    x_copy = pltpu.make_async_copy(x_any, xbuf, local_sem.at[0])
+    x_copy.start()
+    cache_copy = pltpu.make_async_copy(cache_any, cache_buf, local_sem.at[1])
+    cache_copy.start()
+
+    def lane(s):
+        return pl.ds(pl.multiple_of(s * LANES, LANES), LANES)
+
+    my_half = pl.ds(pl.multiple_of(side * half, half), half)
+    other_half = pl.ds(pl.multiple_of((1 - side) * half, half), half)
+
+    own_copies = []
+    for r in range(rounds):
+        own_copies.append(
+            pltpu.make_async_copy(
+                w_any.at[:, pl.ds(r * LANES, LANES)], wbuf.at[r, :, lane(w)], own_sem.at[r]
+            )
+        )
+        own_copies[-1].start()
+
+    barrier = pltpu.get_barrier_semaphore()
+    for d in range(1, n):
+        pl.semaphore_signal(barrier, inc=1, device_id={"wide": lax.rem(w + d, n)})
+    for d in range(1, m_count):
+        pl.semaphore_signal(barrier, inc=1, device_id={"mp": lax.rem(me + d, m_count)})
+    pl.semaphore_signal(barrier, inc=1, device_id={"parts": 1 - side})
+    pl.semaphore_wait(barrier, n - 1 + m_count - 1 + 1)
+
+    def own_send(r, step):
+        sem = right_send if step > 0 else left_send
+        return pltpu.make_async_remote_copy(
+            src_ref=w_any.at[my_half, pl.ds(r * LANES, LANES)],
+            dst_ref=wbuf.at[r, my_half, lane(w)],
+            send_sem=sem.at[r, w],
+            recv_sem=z_recv.at[r, w],
+            device_id={"wide": w + step},
+        )
+
+    def forward(r, s, step):
+        sem = right_send if step > 0 else left_send
+        return pltpu.make_async_remote_copy(
+            src_ref=wbuf.at[r, my_half, lane(s)],
+            dst_ref=wbuf.at[r, my_half, lane(s)],
+            send_sem=sem.at[r, s],
+            recv_sem=z_recv.at[r, s],
+            device_id={"wide": w + step},
+        )
+
+    def across(r, s, rows_at):
+        return pltpu.make_async_remote_copy(
+            src_ref=wbuf.at[r, rows_at, lane(s)],
+            dst_ref=wbuf.at[r, rows_at, lane(s)],
+            send_sem=y_send.at[r, s],
+            recv_sem=y_recv.at[r, s],
+            device_id={"parts": 1 - side},
+        )
+
+    def has_next(step):
+        return w < n - 1 if step > 0 else w > 0
+
+    def has_source(d, step):
+        return w >= d if step > 0 else w + d < n
+
+    def send_own(r):
+        for step in (1, -1):
+
+            @pl.when(has_next(step))
+            def _():
+                own_send(r, step).start()
+
+    def relay(r):
+        for d in range(1, n):
+            for step in (1, -1):
+
+                @pl.when(has_source(d, step))
+                def _():
+                    s = w - d * step
+                    forward(r, s, step).wait_recv()
+
+                    @pl.when(has_next(step))
+                    def _():
+                        forward(r, s, step).start()
+
+                    across(r, s, my_half).start()
+
+    def q_copy(d):
+        return pltpu.make_async_remote_copy(
+            src_ref=q_ref,
+            dst_ref=q_all.at[w],
+            send_sem=q_send.at[d],
+            recv_sem=q_recv.at[w],
+            device_id={"wide": lax.rem(w + d, n)},
+        )
+
+    def q_arrival(d):
+        s = lax.rem(w + d, n)
+        return pltpu.make_async_remote_copy(
+            src_ref=q_ref,
+            dst_ref=q_all.at[s],
+            send_sem=q_send.at[d],
+            recv_sem=q_recv.at[s],
+            device_id={"wide": s},
+        )
+
+    def sq_copy(d, at):
+        return pltpu.make_async_remote_copy(
+            src_ref=squares_here,
+            dst_ref=squares.at[at],
+            send_sem=sq_send.at[d],
+            recv_sem=sq_recv.at[at],
+            device_id={"mp": lax.rem(me + d, m_count)},
+        )
+
+    def rs_copy(r, d, at):
+        target = lax.rem(me + d, m_count)
+        return pltpu.make_async_remote_copy(
+            src_ref=part.at[r, target],
+            dst_ref=gathered.at[r, at],
+            send_sem=rs_send.at[r, d],
+            recv_sem=rs_recv.at[r, at],
+            device_id={"mp": target},
+        )
+
+    def st_copy(h, d, at):
+        target = lax.rem(w + d, n)
+        return pltpu.make_async_remote_copy(
+            src_ref=state_out.at[h, target],
+            dst_ref=state_in.at[h, at],
+            send_sem=st_send.at[h, d],
+            recv_sem=st_recv.at[h, at],
+            device_id={"wide": target},
+        )
+
+    def multiply(r):
+        own_copies[r].wait()
+        for d in range(1, n):
+            across(r, lax.rem(w + d, n), other_half).wait_recv()
+        block = min(128, tokens)
+
+        @pl.loop(0, tokens // block)
+        def _(i):
+            at = pl.ds(pl.multiple_of(i * block, block), block)
+            product = jnp.dot(xbuf[at, :], wbuf[r], preferred_element_type=jnp.float32)
+            for m in range(m_count):
+                part[r, m, at, :] = product[:, m * LANES : (m + 1) * LANES].astype(jnp.bfloat16)
+
+        for d in range(1, m_count):
+            rs_copy(r, d, me).start()
+
+    def reduce(r):
+        total = part[r, me].astype(jnp.float32)
+        for d in range(1, m_count):
+            s = lax.rem(me + d, m_count)
+            rs_copy(r, d, s).wait_recv()
+            total = total + gathered[r, s].astype(jnp.float32)
+        kvbuf[r] = (total * inverse[...]).astype(jnp.bfloat16)
+
+    def pack(out, top, total):
+        at = lax.broadcasted_iota(jnp.int32, (out.shape[0], LANES), 1)
+        return out, jnp.where(at < LANES // 2, top, total)
+
+    def attend_prompt(h):
+        q = q_all[:, h].reshape(n * rows, HD)
+        scores = lax.dot_general(
+            q, kvbuf[2 * h], (((1,), (1,)), ((), ())), preferred_element_type=jnp.float32
+        ) * scale
+        request = lax.broadcasted_iota(jnp.int32, (n * rows, 1), 0) // per_req
+        allowed = label_ref[...] == request
+        scores = jnp.where(allowed, scores, -1e30)
+        top = jnp.max(scores, axis=1, keepdims=True)
+        weights = jnp.where(allowed, jnp.exp(scores - top), 0.0)
+        total = jnp.sum(weights, axis=1, keepdims=True)
+        out = jnp.dot(
+            weights.astype(jnp.bfloat16), kvbuf[2 * h + 1], preferred_element_type=jnp.float32
+        )
+        out, both = pack(out, top, total)
+        state_out[h, :, :, :HD] = out.reshape(n, rows, HD)
+        state_out[h, :, :, HD:] = both.reshape(n, rows, LANES)
+        for d in range(1, n):
+            st_copy(h, d, w).start()
+
+    def attend_cache():
+        step_row = lax.broadcasted_iota(jnp.int32, (per_req, 1), 0) // (per_req // STEPS)
+        for a in range(req_dev):
+            for h in range(heads):
+                q = q_ref[h, a * per_req : (a + 1) * per_req, :]
+                base = 2 * h * HD
+                keys = cache_buf[a, :, base : base + HD]
+                values = cache_buf[a, :, base + HD : base + 2 * HD]
+                over = (((1,), (1,)), ((), ()))
+                sc = lax.dot_general(q, keys, over, preferred_element_type=jnp.float32) * scale
+                ok = lax.broadcasted_iota(jnp.int32, sc.shape, 1) < len_ref[a]
+                sc = jnp.where(ok, sc, -1e30)
+                dk = draft_ref[a, :, base : base + HD]
+                dv = draft_ref[a, :, base + HD : base + 2 * HD]
+                sd = lax.dot_general(q, dk, over, preferred_element_type=jnp.float32) * scale
+                seen = lax.broadcasted_iota(jnp.int32, sd.shape, 1) <= step_row
+                sd = jnp.where(seen, sd, -1e30)
+                top = jnp.maximum(
+                    jnp.max(sc, axis=1, keepdims=True), jnp.max(sd, axis=1, keepdims=True)
+                )
+                wc = jnp.where(ok, jnp.exp(sc - top), 0.0)
+                wd = jnp.where(seen, jnp.exp(sd - top), 0.0)
+                total = jnp.sum(wc, axis=1, keepdims=True) + jnp.sum(wd, axis=1, keepdims=True)
+                out = jnp.dot(wc.astype(jnp.bfloat16), values, preferred_element_type=jnp.float32)
+                out = out + jnp.dot(
+                    wd.astype(jnp.bfloat16), dv, preferred_element_type=jnp.float32
+                )
+                out, both = pack(out, top, total)
+                at = pl.ds(a * per_req, per_req)
+                state_cache[h, at, :HD] = out
+                state_cache[h, at, HD:] = both
+
+    def merge(h):
+        states = [state_cache[h], state_out[h, w]]
+        for d in range(1, n):
+            s = lax.rem(w + d, n)
+            st_copy(h, d, s).wait_recv()
+            states.append(state_in[h, s])
+        tops = [state[:, HD : HD + 1] for state in states]
+        top = functools.reduce(jnp.maximum, tops)
+        total, out = 0.0, 0.0
+        for state, its_top in zip(states, tops):
+            factor = jnp.exp(its_top - top)
+            total = total + factor * state[:, HD + LANES - 1 : HD + LANES]
+            out = out + factor * state[:, :HD]
+        out_ref[h] = (out / total).astype(out_ref.dtype)
+
+    send_own(0)
+    for d in range(1, n):
+        q_copy(d).start()
+    q_all[w] = q_ref[...]
+    x_copy.wait()
+    strip = min(64, tokens)
+
+    @pl.loop(0, tokens // strip)
+    def _(i):
+        at = pl.ds(pl.multiple_of(i * strip, strip), strip)
+        sums = jnp.zeros((strip, LANES), jnp.float32)
+        for c in range(depth // LANES):
+            cut = slice(c * LANES, (c + 1) * LANES)
+            piece = xbuf[at, cut].astype(jnp.float32)
+            sums = sums + piece * piece
+            xbuf[at, cut] = (piece * gain_ref[:, cut]).astype(jnp.bfloat16)
+        squares_here[at, :] = sums
+
+    for d in range(1, m_count):
+        sq_copy(d, me).start()
+
+    for r in range(rounds + 2):
+        if r + 1 < rounds:
+            send_own(r + 1)
+        if r < rounds:
+            relay(r)
+        if r == 0:
+            cache_copy.wait()
+            attend_cache()
+        if r == 1:
+            total = squares_here[...]
+            for d in range(1, m_count):
+                s = lax.rem(me + d, m_count)
+                sq_copy(d, s).wait_recv()
+                total = total + squares[s]
+            mean = jnp.sum(total, axis=1, keepdims=True) / D
+            inverse[...] = jnp.broadcast_to(lax.rsqrt(mean + 1e-05), inverse.shape)
+            for d in range(1, n):
+                q_arrival(d).wait_recv()
+        if 1 <= r <= rounds:
+            multiply(r - 1)
+        if r >= 2:
+            reduce(r - 2)
+            if r % 2 == 1:
+                attend_prompt((r - 3) // 2)
+    for h in range(heads):
+        merge(h)
+
+    for r in range(rounds):
+        for step in (1, -1):
+
+            @pl.when(has_next(step))
+            def _():
+                own_send(r, step).wait_send()
+
+        for d in range(1, n):
+            for step in (1, -1):
+
+                @pl.when(has_source(d, step))
+                def _():
+                    s = w - d * step
+
+                    @pl.when(has_next(step))
+                    def _():
+                        forward(r, s, step).wait_send()
+
+                    across(r, s, my_half).wait_send()
+
+        for d in range(1, m_count):
+            rs_copy(r, d, me).wait_send()
+    for d in range(1, n):
+        q_copy(d).wait_send()
+        for h in range(heads):
+            st_copy(h, d, w).wait_send()
+    for d in range(1, m_count):
+        sq_copy(d, me).wait_send()
+
+
+def on_device_fused(
+    mesh,
+    prompt_states,
+    norm_gain,
+    kv_weight,
+    block_owner,
+    block_request,
+    block_admit,
+    cache_kv,
+    cache_len,
+    queries,
+    draft_kv,
+):
+    n, m_count = mesh.shape["wide"], mesh.shape["mp"]
+    tokens, depth = prompt_states.shape
+    columns = kv_weight.shape[1]
+    req_dev, cached, width = cache_kv.shape
+    if mesh.shape["parts"] != 2 or n != m_count or columns % (2 * HD) or HD != LANES:
+        return on_device(
+            prompt_states,
+            norm_gain,
+            kv_weight,
+            block_owner,
+            block_request,
+            block_admit,
+            cache_kv,
+            cache_len,
+            queries,
+            draft_kv,
+        )
+    rounds = columns // LANES
+    heads = width // (2 * HD)
+    groups = QH // KVH
+    rows = req_dev * STEPS * groups
+    label = jnp.where(block_admit == 1, block_owner[:, 0] * req_dev + block_request, -1)
+    labels = jnp.repeat(label, BLK)[None, :]
+    q = queries.reshape(req_dev, STEPS, heads, groups, HD)
+    q = q.transpose(2, 0, 1, 3, 4).reshape(heads, rows, HD)
+    draft = jnp.pad(draft_kv, ((0, 0), (0, 16 - STEPS), (0, 0)))
+    f32, bf16 = jnp.float32, jnp.bfloat16
+    vmem = pl.BlockSpec(memory_space=pltpu.VMEM)
+    anywhere = pl.BlockSpec(memory_space=pl.ANY)
+    dma = pltpu.SemaphoreType.DMA
+    result = pl.pallas_call(
+        functools.partial(fused_kernel, (n, m_count, rounds, heads, req_dev)),
+        out_shape=jax.ShapeDtypeStruct((heads, rows, HD), bf16),
+        in_specs=[
+            anywhere,
+            vmem,
+            anywhere,
+            vmem,
+            anywhere,
+            pl.BlockSpec(memory_space=pltpu.SMEM),
+            vmem,
+            vmem,
+        ],
+        out_specs=vmem,
+        scratch_shapes=[
+            pltpu.VMEM((tokens, depth), bf16),
+            pltpu.VMEM((rounds, depth, n * LANES), bf16),
+            pltpu.VMEM((rounds, m_count, tokens, LANES), bf16),
+            pltpu.VMEM((rounds, m_count, tokens, LANES), bf16),
+            pltpu.VMEM((tokens, LANES), f32),
+            pltpu.VMEM((m_count, tokens, LANES), f32),
+            pltpu.VMEM((tokens, LANES), f32),
+            pltpu.VMEM((rounds, tokens, LANES), bf16),
+            pltpu.VMEM((req_dev, cached, width), bf16),
+            pltpu.VMEM((n, heads, rows, HD), bf16),
+            pltpu.VMEM((heads, rows, 2 * LANES), f32),
+            pltpu.VMEM((heads, n, rows, 2 * LANES), f32),
+            pltpu.VMEM((heads, n, rows, 2 * LANES), f32),
+            dma((2,)),
+            dma((rounds,)),
+            dma((rounds, n)),
+            dma((rounds, n)),
+            dma((rounds, n)),
+            dma((rounds, n)),
+            dma((rounds, n)),
+            dma((n,)),
+            dma((n,)),
+            dma((m_count,)),
+            dma((m_count,)),
+            dma((rounds, m_count)),
+            dma((rounds, m_count)),
+            dma((heads, n)),
+            dma((heads, n)),
+        ],
+        compiler_params=pltpu.CompilerParams(
+            collective_id=0, has_side_effects=True, vmem_limit_bytes=60 << 20
+        ),
+    )(
+        prompt_states,
+        norm_gain[None, :],
+        kv_weight,
+        labels,
+        cache_kv,
+        cache_len,
+        q,
+        draft,
+    )
+    result = result.reshape(heads, req_dev, STEPS, groups, HD).transpose(1, 2, 0, 3, 4)
+    return result.reshape(req_dev, STEPS, heads * groups * HD)
+
+
 def solution(mesh):
     placed = (
         P(("parts", "wide"), "mp"),
@@ -124,7 +590,7 @@
         P(("parts", "wide"), None, "mp"),
     )
     return jax.shard_map(
-        on_device,
+        functools.partial(on_device_fused, mesh),
         mesh=mesh,
         in_specs=placed,
         out_specs=P(("parts", "wide"), None, "mp"),

time: 252 us -> 111 us (0.44)
  waiting for transfers between devices: 182 us -> 0 us
  Pallas kernels: 0 us -> 105 us
  local copies, waits for them, and re-layouts: 21.3 us -> 4.82 us
  matrix products: 15.6 us -> 0 us
  between operations: 13.6 us -> 0.01 us
  starting transfers between devices: 7.94 us -> 0 us
  blocking collectives: 7.02 us -> 0 us
  other arithmetic: 3.51 us -> 0.69 us
    all_gather x1 -> x0, waiting for transfers between devices: 154 us -> none  [on_device(): lax.all_gather(kv_weight, 'wide', axis=1, tiled=True)]
    pallas_call x0 -> x1, Pallas kernels: none -> 105 us  [on_device_fused(): pl.pallas_call(functools.partial(fused_kernel, (n, m_count, rounds, heads...]
    dot_general x7 -> x0, matrix products: 15.6 us -> none  [the longest x1 9.92 us: on_device(): jnp.dot(scaled, lax.all_gather(kv_weight, 'wide', axis=1, tiled=True), pr...]
    all_to_all x2 -> x0, waiting for transfers between devices: 15.3 us -> none  [the longest x1 15.3 us: on_device(): lax.all_to_all(outgoing, 'wide', split_axis=0, concat_axis=0, tiled=True)]
    reduce_scatter x1 -> x0, waiting for transfers between devices: 12.4 us -> none  [on_device(): lax.psum_scatter(rounded_kv.astype(jnp.bfloat16), 'mp', scatter_dimension...]
    scatter x2 -> x0, local copies, waits for them, and re-layouts: 10 us -> none  [the longest x1 5.34 us: on_device(): jnp.full((wide, capacity), -1, jnp.int32).at[owner, slot].set(tagged)]
    all_to_all x2 -> x0, starting transfers between devices: 7.9 us -> none  [the longest x1 4.55 us: on_device(): lax.all_to_all(outgoing, 'wide', split_axis=0, concat_axis=0, tiled=True)]
    psum x1 -> x0, blocking collectives: 7.02 us -> none  [on_device(): squares = lax.psum(jnp.sum(states * states, axis=1), 'mp')]
  transfers between devices with their start and end apart: 4 -> 0, of which waited for: 3 -> 0; matrix products, arithmetic and copies ran while one was open for 10% -> 0% of each run, Pallas kernels for 0% -> 0%
where the time goes in v1:
time: 111 us; the launch traced here: 110 us
  Pallas kernels  105 us (95%)
  local copies, waits for them, and re-layouts  4.82 us (4%)
    pallas_call x1, Pallas kernels, on_device_fused(): pl.pallas_call(functools.partial(fused_kernel, (n, m_count, rounds, heads...  105 us

profile of v1, /device:TPU:0, one launch (start us, length us, event | category | flops | bytes accessed | tf_op | source)
XLA Modules:
  0.0 110.2 jit_solution(383958587966951571)
XLA Ops:
  0.0 0.7 compare_select_fusion
  0.7 0.1 broadcast_in_dim.12
  0.8 0.6 broadcast_in_dim_reshape.3.label_ref
  1.4 0.8 reshape.14
  2.2 0.6 copy.13
  2.8 1.3 %pad.4.draft_ref = bf16[2,16,512]{2,1,0:T(8,128)(2,1)} pad(bf16[2,4,512]{2,1,0:T(4,128)(2,1)} %param.19, bf16[]{:T(256)} %constant.8.clone.1), padding=0_0x0_12x0_0 | pad | bytes 40962 | tf_op jit(solution)/shard_map/jit(_pad)/pad | solution.py:513
  4.1 104.6 %shard_map.100 = bf16[2,64,128]{2,1,0:T(8,128)(2,1)} custom-call(bf16[512,2048]{1,0:T(8,128)(2,1)} %x_any.1, f32[1,2048]{1,0:T(1,128)} %bitcast.15, bf16[2048,512]{1,0:T(8,128)(2,1)} %w_any.1, s32[1,512]{1,0:T(1,128)} %broadcast_in_dim_reshape.3.label_ref, bf16[2,2048,512]{2,1,0:T(8,128)(2,1)} %cache_any.1, s32[2]{0:T(128)} %len_ref.1, ...), custom_call_target="tpu_custom_call" | custom-call | tf_op jit(solution)/shard_map/pallas_call | solution.py:518
  108.8 0.8 copy.14
  109.5 0.6 reshape.17

commit v2 on v1

--- a/solution.py
+++ b/solution.py
@@ -121,10 +121,12 @@
     x_any,
     gain_ref,
     w_any,
-    label_ref,
+    owner_ref,
+    request_ref,
+    admit_ref,
     cache_any,
     len_ref,
-    q_ref,
+    query_ref,
     draft_ref,
     out_ref,
     xbuf,
@@ -136,10 +138,16 @@
     inverse,
     kvbuf,
     cache_buf,
+    q_here,
     q_all,
-    state_cache,
-    state_out,
-    state_in,
+    labels,
+    prob,
+    cache_out,
+    cache_ml,
+    out_send,
+    out_recv,
+    ml_send,
+    ml_recv,
     local_sem,
     own_sem,
     right_send,
@@ -155,14 +163,18 @@
     rs_recv,
     st_send,
     st_recv,
+    mls_send,
+    mls_recv,
 ):
-    n, m_count, rounds, heads, req_dev = sizes
+    n, m_count, rounds, heads, req_dev, pieces = sizes
     w = lax.axis_index("wide")
     me = lax.axis_index("mp")
     side = lax.axis_index("parts")
     tokens, depth = xbuf.shape
     half = depth // 2
-    rows = q_ref.shape[1]
+    rows = q_here.shape[1]
+    groups = rows // (req_dev * STEPS)
+    piece = half // pieces
     per_req = rows // req_dev
     scale = 1.0 / math.sqrt(HD)
 
@@ -174,8 +186,8 @@
     def lane(s):
         return pl.ds(pl.multiple_of(s * LANES, LANES), LANES)
 
-    my_half = pl.ds(pl.multiple_of(side * half, half), half)
-    other_half = pl.ds(pl.multiple_of((1 - side) * half, half), half)
+    def rows_of(whose, k):
+        return pl.ds(pl.multiple_of(whose * half + k * piece, piece), piece)
 
     own_copies = []
     for r in range(rounds):
@@ -194,32 +206,32 @@
     pl.semaphore_signal(barrier, inc=1, device_id={"parts": 1 - side})
     pl.semaphore_wait(barrier, n - 1 + m_count - 1 + 1)
 
-    def own_send(r, step):
+    def own_send(r, k, step):
         sem = right_send if step > 0 else left_send
         return pltpu.make_async_remote_copy(
-            src_ref=w_any.at[my_half, pl.ds(r * LANES, LANES)],
-            dst_ref=wbuf.at[r, my_half, lane(w)],
-            send_sem=sem.at[r, w],
-            recv_sem=z_recv.at[r, w],
+            src_ref=w_any.at[rows_of(side, k), pl.ds(r * LANES, LANES)],
+            dst_ref=wbuf.at[r, rows_of(side, k), lane(w)],
+            send_sem=sem.at[r * pieces + k, w],
+            recv_sem=z_recv.at[r * pieces + k, w],
             device_id={"wide": w + step},
         )
 
-    def forward(r, s, step):
+    def forward(r, k, s, step):
         sem = right_send if step > 0 else left_send
         return pltpu.make_async_remote_copy(
-            src_ref=wbuf.at[r, my_half, lane(s)],
-            dst_ref=wbuf.at[r, my_half, lane(s)],
-            send_sem=sem.at[r, s],
-            recv_sem=z_recv.at[r, s],
+            src_ref=wbuf.at[r, rows_of(side, k), lane(s)],
+            dst_ref=wbuf.at[r, rows_of(side, k), lane(s)],
+            send_sem=sem.at[r * pieces + k, s],
+            recv_sem=z_recv.at[r * pieces + k, s],
             device_id={"wide": w + step},
         )
 
-    def across(r, s, rows_at):
-        return pltpu.make_async_remote_copy(
-            src_ref=wbuf.at[r, rows_at, lane(s)],
-            dst_ref=wbuf.at[r, rows_at, lane(s)],
-            send_sem=y_send.at[r, s],
-            recv_sem=y_recv.at[r, s],
+    def across(r, k, s, whose):
+        return pltpu.make_async_remote_copy(
+            src_ref=wbuf.at[r, rows_of(whose, k), lane(s)],
+            dst_ref=wbuf.at[r, rows_of(whose, k), lane(s)],
+            send_sem=y_send.at[r * pieces + k, s],
+            recv_sem=y_recv.at[r * pieces + k, s],
             device_id={"parts": 1 - side},
         )
 
@@ -229,31 +241,31 @@
     def has_source(d, step):
         return w >= d if step > 0 else w + d < n
 
-    def send_own(r):
+    def send_own(r, k):
         for step in (1, -1):
 
             @pl.when(has_next(step))
             def _():
-                own_send(r, step).start()
-
-    def relay(r):
+                own_send(r, k, step).start()
+
+    def relay(r, k):
         for d in range(1, n):
             for step in (1, -1):
 
                 @pl.when(has_source(d, step))
                 def _():
                     s = w - d * step
-                    forward(r, s, step).wait_recv()
+                    forward(r, k, s, step).wait_recv()
 
                     @pl.when(has_next(step))
                     def _():
-                        forward(r, s, step).start()
-
-                    across(r, s, my_half).start()
+                        forward(r, k, s, step).start()
+
+                    across(r, k, s, side).start()
 
     def q_copy(d):
         return pltpu.make_async_remote_copy(
-            src_ref=q_ref,
+            src_ref=q_here,
             dst_ref=q_all.at[w],
             send_sem=q_send.at[d],
             recv_sem=q_recv.at[w],
@@ -263,7 +275,7 @@
     def q_arrival(d):
         s = lax.rem(w + d, n)
         return pltpu.make_async_remote_copy(
-            src_ref=q_ref,
+            src_ref=q_here,
             dst_ref=q_all.at[s],
             send_sem=q_send.at[d],
             recv_sem=q_recv.at[s],
@@ -289,20 +301,23 @@
             device_id={"mp": target},
         )
 
-    def st_copy(h, d, at):
+    def state_copy(h, d, at, values):
         target = lax.rem(w + d, n)
-        return pltpu.make_async_remote_copy(
-            src_ref=state_out.at[h, target],
-            dst_ref=state_in.at[h, at],
-            send_sem=st_send.at[h, d],
-            recv_sem=st_recv.at[h, at],
+        source, sink = (out_send, out_recv) if values else (ml_send, ml_recv)
+        gone, come = (st_send, st_recv) if values else (mls_send, mls_recv)
+        return pltpu.make_async_remote_copy(
+            src_ref=source.at[h, target],
+            dst_ref=sink.at[h, at],
+            send_sem=gone.at[h, d],
+            recv_sem=come.at[h, at],
             device_id={"wide": target},
         )
 
     def multiply(r):
         own_copies[r].wait()
-        for d in range(1, n):
-            across(r, lax.rem(w + d, n), other_half).wait_recv()
+        for k in range(pieces):
+            for d in range(1, n):
+                across(r, k, lax.rem(w + d, n), 1 - side).wait_recv()
         block = min(128, tokens)
 
         @pl.loop(0, tokens // block)
@@ -323,81 +338,114 @@
             total = total + gathered[r, s].astype(jnp.float32)
         kvbuf[r] = (total * inverse[...]).astype(jnp.bfloat16)
 
-    def pack(out, top, total):
-        at = lax.broadcasted_iota(jnp.int32, (out.shape[0], LANES), 1)
-        return out, jnp.where(at < LANES // 2, top, total)
-
-    def attend_prompt(h):
+    def pack(top, total):
+        at = lax.broadcasted_iota(jnp.int32, (top.shape[0], LANES), 1)
+        return jnp.where(at < LANES // 2, top, total)
+
+    def attend_scores(h):
         q = q_all[:, h].reshape(n * rows, HD)
         scores = lax.dot_general(
             q, kvbuf[2 * h], (((1,), (1,)), ((), ())), preferred_element_type=jnp.float32
         ) * scale
         request = lax.broadcasted_iota(jnp.int32, (n * rows, 1), 0) // per_req
-        allowed = label_ref[...] == request
+        allowed = labels[0:1, :] == request
         scores = jnp.where(allowed, scores, -1e30)
         top = jnp.max(scores, axis=1, keepdims=True)
         weights = jnp.where(allowed, jnp.exp(scores - top), 0.0)
         total = jnp.sum(weights, axis=1, keepdims=True)
-        out = jnp.dot(
-            weights.astype(jnp.bfloat16), kvbuf[2 * h + 1], preferred_element_type=jnp.float32
-        )
-        out, both = pack(out, top, total)
-        state_out[h, :, :, :HD] = out.reshape(n, rows, HD)
-        state_out[h, :, :, HD:] = both.reshape(n, rows, LANES)
+        prob[h] = weights.astype(jnp.bfloat16)
+        ml_send[h] = pack(top, total).reshape(n, rows, LANES)
         for d in range(1, n):
-            st_copy(h, d, w).start()
-
-    def attend_cache():
-        step_row = lax.broadcasted_iota(jnp.int32, (per_req, 1), 0) // (per_req // STEPS)
-        for a in range(req_dev):
-            for h in range(heads):
-                q = q_ref[h, a * per_req : (a + 1) * per_req, :]
-                base = 2 * h * HD
-                keys = cache_buf[a, :, base : base + HD]
-                values = cache_buf[a, :, base + HD : base + 2 * HD]
-                over = (((1,), (1,)), ((), ()))
-                sc = lax.dot_general(q, keys, over, preferred_element_type=jnp.float32) * scale
-                ok = lax.broadcasted_iota(jnp.int32, sc.shape, 1) < len_ref[a]
-                sc = jnp.where(ok, sc, -1e30)
-                dk = draft_ref[a, :, base : base + HD]
-                dv = draft_ref[a, :, base + HD : base + 2 * HD]
-                sd = lax.dot_general(q, dk, over, preferred_element_type=jnp.float32) * scale
-                seen = lax.broadcasted_iota(jnp.int32, sd.shape, 1) <= step_row
-                sd = jnp.where(seen, sd, -1e30)
-                top = jnp.maximum(
-                    jnp.max(sc, axis=1, keepdims=True), jnp.max(sd, axis=1, keepdims=True)
-                )
-                wc = jnp.where(ok, jnp.exp(sc - top), 0.0)
-                wd = jnp.where(seen, jnp.exp(sd - top), 0.0)
-                total = jnp.sum(wc, axis=1, keepdims=True) + jnp.sum(wd, axis=1, keepdims=True)
-                out = jnp.dot(wc.astype(jnp.bfloat16), values, preferred_element_type=jnp.float32)
-                out = out + jnp.dot(
-                    wd.astype(jnp.bfloat16), dv, preferred_element_type=jnp.float32
-                )
-                out, both = pack(out, top, total)
-                at = pl.ds(a * per_req, per_req)
-                state_cache[h, at, :HD] = out
-                state_cache[h, at, HD:] = both
-
-    def merge(h):
-        states = [state_cache[h], state_out[h, w]]
+            state_copy(h, d, w, False).start()
+
+    def attend_values(h):
+        out = jnp.dot(prob[h], kvbuf[2 * h + 1], preferred_element_type=jnp.float32)
+        out_send[h] = out.astype(jnp.bfloat16).reshape(n, rows, HD)
+        for d in range(1, n):
+            state_copy(h, d, w, True).start()
+
+    def attend_cache(a):
+        step_row = lax.rem(lax.broadcasted_iota(jnp.int32, (per_req, 1), 0), STEPS)
+        drafted = draft_ref[a].astype(jnp.float32)
+        drafted = jnp.concatenate(
+            [drafted, jnp.zeros((16 - STEPS, drafted.shape[1]), jnp.float32)], axis=0
+        ).astype(jnp.bfloat16)
+        for h in range(heads):
+            q = q_here[h, a * per_req : (a + 1) * per_req, :]
+            base = 2 * h * HD
+            keys = cache_buf[a, :, base : base + HD]
+            values = cache_buf[a, :, base + HD : base + 2 * HD]
+            over = (((1,), (1,)), ((), ()))
+            sc = lax.dot_general(q, keys, over, preferred_element_type=jnp.float32) * scale
+            ok = lax.broadcasted_iota(jnp.int32, sc.shape, 1) < len_ref[a]
+            sc = jnp.where(ok, sc, -1e30)
+            dk = drafted[:, base : base + HD]
+            dv = drafted[:, base + HD : base + 2 * HD]
+            sd = lax.dot_general(q, dk, over, preferred_element_type=jnp.float32) * scale
+            seen = lax.broadcasted_iota(jnp.int32, sd.shape, 1) <= step_row
+            sd = jnp.where(seen, sd, -1e30)
+            top = jnp.maximum(
+                jnp.max(sc, axis=1, keepdims=True), jnp.max(sd, axis=1, keepdims=True)
+            )
+            wc = jnp.where(ok, jnp.exp(sc - top), 0.0)
+            wd = jnp.where(seen, jnp.exp(sd - top), 0.0)
+            total = jnp.sum(wc, axis=1, keepdims=True) + jnp.sum(wd, axis=1, keepdims=True)
+            out = jnp.dot(wc.astype(jnp.bfloat16), values, preferred_element_type=jnp.float32)
+            out = out + jnp.dot(wd.astype(jnp.bfloat16), dv, preferred_element_type=jnp.float32)
+            at = pl.ds(a * per_req, per_req)
+            cache_out[h, at, :] = out
+            cache_ml[h, at, :] = pack(top, total)
+
+    def factors(h):
+        stats = [cache_ml[h], ml_send[h, w]]
         for d in range(1, n):
             s = lax.rem(w + d, n)
-            st_copy(h, d, s).wait_recv()
-            states.append(state_in[h, s])
-        tops = [state[:, HD : HD + 1] for state in states]
+            state_copy(h, d, s, False).wait_recv()
+            stats.append(ml_recv[h, s])
+        tops = [each[:, 0:1] for each in stats]
         top = functools.reduce(jnp.maximum, tops)
-        total, out = 0.0, 0.0
-        for state, its_top in zip(states, tops):
-            factor = jnp.exp(its_top - top)
-            total = total + factor * state[:, HD + LANES - 1 : HD + LANES]
-            out = out + factor * state[:, :HD]
-        out_ref[h] = (out / total).astype(out_ref.dtype)
-
-    send_own(0)
+        scaled = [jnp.exp(each - top) for each in tops]
+        total = sum(f * each[:, LANES - 1 : LANES] for f, each in zip(scaled, stats))
+        return [f / total for f in scaled]
+
+    def merge(h, share):
+        out = share[0] * cache_out[h] + share[1] * out_send[h, w].astype(jnp.float32)
+        for d in range(1, n):
+            s = lax.rem(w + d, n)
+            state_copy(h, d, s, True).wait_recv()
+            out = out + share[d + 1] * out_recv[h, s].astype(jnp.float32)
+        for a in range(req_dev):
+            for g in range(groups):
+                at = (a * groups + g) * STEPS
+                cut = slice((h * groups + g) * HD, (h * groups + g + 1) * HD)
+                out_ref[a, :, cut] = out[at : at + STEPS, :].astype(out_ref.dtype)
+
+    send_own(0, 0)
+    for h in range(heads):
+        q_here[h] = jnp.concatenate(
+            [
+                query_ref[a, :, (h * groups + g) * HD : (h * groups + g + 1) * HD].astype(
+                    jnp.float32
+                )
+                for a in range(req_dev)
+                for g in range(groups)
+            ],
+            axis=0,
+        ).astype(jnp.bfloat16)
     for d in range(1, n):
         q_copy(d).start()
-    q_all[w] = q_ref[...]
+    q_all[w] = q_here[...]
+    blocks = owner_ref.shape[0]
+    shape = (blocks, blocks)
+    same = lax.broadcasted_iota(jnp.int32, shape, 0) == lax.broadcasted_iota(jnp.int32, shape, 1)
+    request = jnp.sum(jnp.where(same, request_ref[...], 0), axis=1, keepdims=True)
+    admit = jnp.sum(jnp.where(same, admit_ref[...], 0), axis=1, keepdims=True)
+    label = jnp.where(admit == 1, owner_ref[...] * req_dev + request, -1)
+    shape = (blocks, tokens)
+    block_of = lax.broadcasted_iota(jnp.int32, shape, 1) // (tokens // blocks)
+    inside = block_of == lax.broadcasted_iota(jnp.int32, shape, 0)
+    row = jnp.sum(jnp.where(inside, label, 0), axis=0, keepdims=True)
+    labels[...] = jnp.broadcast_to(row, labels.shape)
     x_copy.wait()
     strip = min(64, tokens)
 
@@ -415,39 +463,59 @@
     for d in range(1, m_count):
         sq_copy(d, me).start()
 
-    for r in range(rounds + 2):
-        if r + 1 < rounds:
-            send_own(r + 1)
-        if r < rounds:
-            relay(r)
-        if r == 0:
-            cache_copy.wait()
-            attend_cache()
+    order = [(r, k) for r in range(rounds) for k in range(pieces)]
+
+    def stats():
+        total = squares_here[...]
+        for d in range(1, m_count):
+            s = lax.rem(me + d, m_count)
+            sq_copy(d, s).wait_recv()
+            total = total + squares[s]
+        mean = jnp.sum(total, axis=1, keepdims=True) / D
+        inverse[...] = jnp.broadcast_to(lax.rsqrt(mean + 1e-05), inverse.shape)
+        for d in range(1, n):
+            q_arrival(d).wait_recv()
+
+    def collect(r):
+        reduce(r)
+        if r % 2 == 0:
+            attend_scores(r // 2)
+        else:
+            attend_values(r // 2)
+
+    work = {}
+
+    def plan(r, k, job):
+        work.setdefault((r, min(k, pieces - 1)), []).append(job)
+
+    for a in range(req_dev):
+        plan(0, a, functools.partial(attend_cache, a))
+    for r in range(1, rounds):
+        plan(r, 0, functools.partial(multiply, r - 1))
         if r == 1:
-            total = squares_here[...]
-            for d in range(1, m_count):
-                s = lax.rem(me + d, m_count)
-                sq_copy(d, s).wait_recv()
-                total = total + squares[s]
-            mean = jnp.sum(total, axis=1, keepdims=True) / D
-            inverse[...] = jnp.broadcast_to(lax.rsqrt(mean + 1e-05), inverse.shape)
-            for d in range(1, n):
-                q_arrival(d).wait_recv()
-        if 1 <= r <= rounds:
-            multiply(r - 1)
-        if r >= 2:
-            reduce(r - 2)
-            if r % 2 == 1:
-                attend_prompt((r - 3) // 2)
+            plan(r, 0, stats)
+        else:
+            plan(r, 1, functools.partial(collect, r - 2))
+    cache_copy.wait()
+    for i, (r, k) in enumerate(order):
+        if i + 1 < len(order):
+            send_own(*order[i + 1])
+        relay(r, k)
+        for job in work.get((r, k), []):
+            job()
+    multiply(rounds - 1)
+    for r in range(max(rounds - 2, 0), rounds):
+        collect(r)
+    shares = [factors(h) for h in range(heads)]
     for h in range(heads):
-        merge(h)
-
-    for r in range(rounds):
+        merge(h, shares[h])
+
+    for r, k in order:
         for step in (1, -1):
 
             @pl.when(has_next(step))
             def _():
-                own_send(r, step).wait_send()
+                own_send(r, k, step).wait_send()
 
         for d in range(1, n):
             for step in (1, -1):
@@ -458,16 +526,18 @@
 
                     @pl.when(has_next(step))
                     def _():
-                        forward(r, s, step).wait_send()
-
-                    across(r, s, my_half).wait_send()
-
+                        forward(r, k, s, step).wait_send()
+
+                    across(r, k, s, side).wait_send()
+
+    for r in range(rounds):
         for d in range(1, m_count):
             rs_copy(r, d, me).wait_send()
     for d in range(1, n):
         q_copy(d).wait_send()
         for h in range(heads):
-            st_copy(h, d, w).wait_send()
+            state_copy(h, d, w, False).wait_send()
+            state_copy(h, d, w, True).wait_send()
     for d in range(1, m_count):
         sq_copy(d, me).wait_send()
 
@@ -506,22 +576,20 @@
     heads = width // (2 * HD)
     groups = QH // KVH
     rows = req_dev * STEPS * groups
-    label = jnp.where(block_admit == 1, block_owner[:, 0] * req_dev + block_request, -1)
-    labels = jnp.repeat(label, BLK)[None, :]
-    q = queries.reshape(req_dev, STEPS, heads, groups, HD)
-    q = q.transpose(2, 0, 1, 3, 4).reshape(heads, rows, HD)
-    draft = jnp.pad(draft_kv, ((0, 0), (0, 16 - STEPS), (0, 0)))
+    pieces = 2
     f32, bf16 = jnp.float32, jnp.bfloat16
     vmem = pl.BlockSpec(memory_space=pltpu.VMEM)
     anywhere = pl.BlockSpec(memory_space=pl.ANY)
     dma = pltpu.SemaphoreType.DMA
-    result = pl.pallas_call(
-        functools.partial(fused_kernel, (n, m_count, rounds, heads, req_dev)),
-        out_shape=jax.ShapeDtypeStruct((heads, rows, HD), bf16),
+    return pl.pallas_call(
+        functools.partial(fused_kernel, (n, m_count, rounds, heads, req_dev, pieces)),
+        out_shape=jax.ShapeDtypeStruct(queries.shape, bf16),
         in_specs=[
             anywhere,
             vmem,
             anywhere,
+            vmem,
+            vmem,
             vmem,
             anywhere,
             pl.BlockSpec(memory_space=pltpu.SMEM),
@@ -539,23 +607,31 @@
             pltpu.VMEM((tokens, LANES), f32),
             pltpu.VMEM((rounds, tokens, LANES), bf16),
             pltpu.VMEM((req_dev, cached, width), bf16),
+            pltpu.VMEM((heads, rows, HD), bf16),
             pltpu.VMEM((n, heads, rows, HD), bf16),
-            pltpu.VMEM((heads, rows, 2 * LANES), f32),
-            pltpu.VMEM((heads, n, rows, 2 * LANES), f32),
-            pltpu.VMEM((heads, n, rows, 2 * LANES), f32),
+            pltpu.VMEM((8, tokens), jnp.int32),
+            pltpu.VMEM((heads, n * rows, tokens), bf16),
+            pltpu.VMEM((heads, rows, HD), f32),
+            pltpu.VMEM((heads, rows, LANES), f32),
+            pltpu.VMEM((heads, n, rows, HD), bf16),
+            pltpu.VMEM((heads, n, rows, HD), bf16),
+            pltpu.VMEM((heads, n, rows, LANES), f32),
+            pltpu.VMEM((heads, n, rows, LANES), f32),
             dma((2,)),
             dma((rounds,)),
-            dma((rounds, n)),
-            dma((rounds, n)),
-            dma((rounds, n)),
-            dma((rounds, n)),
-            dma((rounds, n)),
+            dma((rounds * pieces, n)),
+            dma((rounds * pieces, n)),
+            dma((rounds * pieces, n)),
+            dma((rounds * pieces, n)),
+            dma((rounds * pieces, n)),
             dma((n,)),
             dma((n,)),
             dma((m_count,)),
             dma((m_count,)),
             dma((rounds, m_count)),
             dma((rounds, m_count)),
+            dma((heads, n)),
+            dma((heads, n)),
             dma((heads, n)),
             dma((heads, n)),
         ],
@@ -566,14 +642,14 @@
         prompt_states,
         norm_gain[None, :],
         kv_weight,
-        labels,
+        block_owner,
+        block_request[None, :],
+        block_admit[None, :],
         cache_kv,
         cache_len,
-        q,
-        draft,
-    )
-    result = result.reshape(heads, req_dev, STEPS, groups, HD).transpose(1, 2, 0, 3, 4)
-    return result.reshape(req_dev, STEPS, heads * groups * HD)
+        queries,
+        draft_kv,
+    )
 
 
 def solution(mesh):

time: 111 us -> 104 us (0.937)
  Pallas kernels: 105 us -> 101 us
  local copies, waits for them, and re-layouts: 4.82 us -> 2.72 us
    pallas_call x1, Pallas kernels: 105 us -> 101 us  [on_device_fused(): pl.pallas_call(functools.partial(fused_kernel, (n, m_count, rounds, heads...]
    unnamed x0 -> x2, local copies, waits for them, and re-layouts: none -> 2.72 us
    reshape x3 -> x0, local copies, waits for them, and re-layouts: 2.04 us -> none  [the longest x2 1.4 us: on_device_fused(): q = queries.reshape(req_dev, STEPS, heads, groups, HD)]
    pad x1 -> x0, local copies, waits for them, and re-layouts: 1.3 us -> none  [on_device_fused(): draft = jnp.pad(draft_kv, ((0, 0), (0, 16 - STEPS), (0, 0)))]
where the time goes in v2:
time: 104 us
  Pallas kernels  101 us (97%)
  local copies, waits for them, and re-layouts  2.72 us (3%)
    pallas_call x1, Pallas kernels, on_device_fused(): pl.pallas_call(functools.partial(fused_kernel, (n, m_count, rounds, heads...  101 us
    unnamed x2, local copies, waits for them, and re-layouts  2.72 us

profile of v2, /device:TPU:0, one launch (start us, length us, event | category | flops | bytes accessed | tf_op | source)
XLA Modules:
  0.0 104.0 jit_solution(11279124830105719539)
XLA Ops:
  0.0 1.3 %copy.11.owner_ref = s32[32,1]{1,0:T(8,128)} copy(s32[32,1]{0,1:T(1,128)} %param.13) | data formatting | bytes 256 | tf_op args[3]
  1.3 101.3 %shard_map.100 = bf16[2,4,2048]{2,1,0:T(4,128)(2,1)} custom-call(bf16[512,2048]{1,0:T(8,128)(2,1)} %x_any.1, f32[1,2048]{1,0:T(1,128)} %bitcast.3, bf16[2048,512]{1,0:T(8,128)(2,1)} %w_any.1, s32[32,1]{1,0:T(8,128)} %copy.11.owner_ref, s32[1,32]{1,0:T(1,128)} %bitcast.4, s32[1,32]{1,0:T(1,128)} %bitcast.5, bf16[2,2048,512]{2,1,0:T(8,128)(2,1)} %cache_any.1, ...), custom_call_target="tpu_custom_call" | custom-call | tf_op jit(solution)/shard_map/pallas_call | solution.py:584
  102.6 1.4 %copy.13 = bf16[2,4,2048]{2,1,0:T(4,128)(2,1)} copy(bf16[2,4,2048]{2,1,0:T(4,128)(2,1)} %shard_map.100) | data formatting | bytes 65536

commit v3 on v2

--- a/solution.py
+++ b/solution.py
@@ -327,7 +327,7 @@
             for m in range(m_count):
                 part[r, m, at, :] = product[:, m * LANES : (m + 1) * LANES].astype(jnp.bfloat16)
 
-        for d in range(1, m_count):
+        for d in (*range(2, m_count), 1):
             rs_copy(r, d, me).start()
 
     def reduce(r):
@@ -354,7 +354,13 @@
         weights = jnp.where(allowed, jnp.exp(scores - top), 0.0)
         total = jnp.sum(weights, axis=1, keepdims=True)
         prob[h] = weights.astype(jnp.bfloat16)
-        ml_send[h] = pack(top, total).reshape(n, rows, LANES)
+        both = pack(top, total)
+        at = lax.broadcasted_iota(jnp.int32, both.shape, 1)
+        mine = lax.rem(lax.broadcasted_iota(jnp.int32, both.shape, 0), rows)
+        both = jnp.where(lax.rem(at, LANES // 2) == mine, both, 0.0)
+        for o in range(n):
+            row = jnp.sum(both[o * rows : (o + 1) * rows], axis=0, keepdims=True)
+            ml_send[h, o] = jnp.broadcast_to(row, ml_send.shape[2:])
         for d in range(1, n):
             state_copy(h, d, w, False).start()
 
@@ -396,16 +402,24 @@
             cache_out[h, at, :] = out
             cache_ml[h, at, :] = pack(top, total)
 
+    def unpack(packed):
+        wide_row = jnp.broadcast_to(packed[0:1, :], (rows, LANES))
+        at = lax.broadcasted_iota(jnp.int32, wide_row.shape, 1)
+        mine = lax.broadcasted_iota(jnp.int32, wide_row.shape, 0)
+        return [
+            jnp.sum(jnp.where(at == mine + off, wide_row, 0.0), axis=1, keepdims=True)
+            for off in (0, LANES // 2)
+        ]
+
     def factors(h):
-        stats = [cache_ml[h], ml_send[h, w]]
+        stats = [(cache_ml[h, :, 0:1], cache_ml[h, :, LANES - 1 : LANES]), unpack(ml_send[h, w])]
         for d in range(1, n):
             s = lax.rem(w + d, n)
             state_copy(h, d, s, False).wait_recv()
-            stats.append(ml_recv[h, s])
-        tops = [each[:, 0:1] for each in stats]
-        top = functools.reduce(jnp.maximum, tops)
-        scaled = [jnp.exp(each - top) for each in tops]
-        total = sum(f * each[:, LANES - 1 : LANES] for f, each in zip(scaled, stats))
+            stats.append(unpack(ml_recv[h, s]))
+        top = functools.reduce(jnp.maximum, [each[0] for each in stats])
+        scaled = [jnp.exp(each[0] - top) for each in stats]
+        total = sum(f * each[1] for f, each in zip(scaled, stats))
         return [f / total for f in scaled]
 
     def merge(h, share):
@@ -559,7 +573,10 @@
     tokens, depth = prompt_states.shape
     columns = kv_weight.shape[1]
     req_dev, cached, width = cache_kv.shape
-    if mesh.shape["parts"] != 2 or n != m_count or columns % (2 * HD) or HD != LANES:
+    groups = QH // KVH
+    rows = req_dev * STEPS * groups
+    plain = mesh.shape["parts"] != 2 or n != m_count or columns % (2 * HD) or HD != LANES
+    if plain or 2 * rows > LANES:
         return on_device(
             prompt_states,
             norm_gain,
@@ -574,8 +591,6 @@
         )
     rounds = columns // LANES
     heads = width // (2 * HD)
-    groups = QH // KVH
-    rows = req_dev * STEPS * groups
     pieces = 2
     f32, bf16 = jnp.float32, jnp.bfloat16
     vmem = pl.BlockSpec(memory_space=pltpu.VMEM)
@@ -615,8 +630,8 @@
             pltpu.VMEM((heads, rows, LANES), f32),
             pltpu.VMEM((heads, n, rows, HD), bf16),
             pltpu.VMEM((heads, n, rows, HD), bf16),
-            pltpu.VMEM((heads, n, rows, LANES), f32),
-            pltpu.VMEM((heads, n, rows, LANES), f32),
+            pltpu.VMEM((heads, n, 8, LANES), f32),
+            pltpu.VMEM((heads, n, 8, LANES), f32),
             dma((2,)),
             dma((rounds,)),
             dma((rounds * pieces, n)),

time: 104 us -> 102 us (0.981)
  Pallas kernels: 101 us -> 99.4 us
    pallas_call x1, Pallas kernels: 101 us -> 99.4 us  [on_device_fused(): pl.pallas_call(functools.partial(fused_kernel, (n, m_count, rounds, heads...]
where the time goes in v3:
time: 102 us
  Pallas kernels  99.4 us (97%)
  local copies, waits for them, and re-layouts  2.72 us (3%)
    pallas_call x1, Pallas kernels, on_device_fused(): pl.pallas_call(functools.partial(fused_kernel, (n, m_count, rounds, heads...  99.4 us
    unnamed x2, local copies, waits for them, and re-layouts  2.72 us

profile of v3, /device:TPU:0, one launch (start us, length us, event | category | flops | bytes accessed | tf_op | source)
XLA Modules:
  0.0 102.2 jit_solution(16914639972360112707)
XLA Ops:
  0.0 1.3 %copy.11.owner_ref = s32[32,1]{1,0:T(8,128)} copy(s32[32,1]{0,1:T(1,128)} %param.13) | data formatting | bytes 256 | tf_op args[3]
  1.3 99.4 %shard_map.100 = bf16[2,4,2048]{2,1,0:T(4,128)(2,1)} custom-call(bf16[512,2048]{1,0:T(8,128)(2,1)} %x_any.1, f32[1,2048]{1,0:T(1,128)} %bitcast.3, bf16[2048,512]{1,0:T(8,128)(2,1)} %w_any.1, s32[32,1]{1,0:T(8,128)} %copy.11.owner_ref, s32[1,32]{1,0:T(1,128)} %bitcast.4, s32[1,32]{1,0:T(1,128)} %bitcast.5, bf16[2,2048,512]{2,1,0:T(8,128)(2,1)} %cache_any.1, ...), custom_call_target="tpu_custom_call" | custom-call | tf_op jit(solution)/shard_map/pallas_call | solution.py:599
  100.8 1.4 %copy.13 = bf16[2,4,2048]{2,1,0:T(4,128)(2,1)} copy(bf16[2,4,2048]{2,1,0:T(4,128)(2,1)} %shard_map.100) | data formatting | bytes 65536
